TPU v7x, 32 devices: a whole 2x2x4 slice. The times are simulated.
32 devices in a mesh: tomo: 4 (over y, x), brick: 8 (over z, core).
Axes of the slice: x: 2, y: 2, z: 4, core: 2. Of those that a mesh axis runs over, the one named last changes fastest.
Arguments:
- features: bfloat16 [4, 64, 512, 128], P('tomo', 'brick'), may hold values from -6 to 6
- weight: bfloat16 [27, 128, 128], replicated, may hold values from -0.109375 to 0.109375
- cotangent: bfloat16 [4, 64, 512, 128], P('tomo', 'brick'), may hold values from -6 to 6
- brick_pos: int32 [4, 64], P('tomo', 'brick'), may hold values from 0 to 7, as said below
- brick_count: int32 [4, 8], P('tomo', 'brick'), may hold values from 3 to 8, as said below
Outputs:
- output: bfloat16 [4, 64, 512, 128], P('tomo', 'brick')
- input_grad: bfloat16 [4, 64, 512, 128], P('tomo', 'brick')
- weight_grad: float32 [27, 128, 128], replicated
Inputs may be any that keep to these rules, and one draw needn't show every extreme that they name: `brick_count`: in every crop some device has all 8 positions occupied. `brick_pos`: the 8 slots of one device hold each position 0 to 7 once: first the occupied positions in increasing order, then the empty ones in increasing order.
All inputs are finite; a program needn't handle non-finite values.
Results may differ from a plain program's by a relative error of at most 0.001.
Values may be sent and summed in bfloat16 or wider, within the bound.
A program may use at most 128 MiB of HBM per device.

v0:
```python
import functools
import math

import jax
import jax.numpy as jnp
from jax import lax
from jax.experimental import pallas as pl
from jax.experimental.pallas import tpu as pltpu
from jax.sharding import PartitionSpec as P

BE = 8
MESH = pl.DeviceIdType.MESH
UNIT = 8


def coords_of(index, levels):
    out = []
    for bit in (2, 1, 0):
        c = 0
        for level in range(levels):
            c = c + lax.rem(index // (1 << (3 * level + bit)), 2) * (1 << level)
        out.append(c)
    return out


def index_of(coords, levels):
    i = 0
    for bit, c in zip((2, 1, 0), coords):
        for level in range(levels):
            i = i + lax.rem(c // (1 << level), 2) * (1 << (3 * level + bit))
    return i


def kernel(
    factor, tb, bb, streams,
    pos_ref, cnt_ref, f_ref, g_ref, w_ref,
    out_ref, dx_ref, tot,
    pad, zs, zr, wx, gt, obuf, src, land,
    hsend, hrecv, rsend, rrecv, gsend, grecv,
):
    e = 2 * BE
    half = e // 2
    ch = f_ref.shape[-1]
    levels = bb // 3
    side = 1 << levels
    tomo = lax.axis_index("tomo")
    brick = lax.axis_index("brick")
    here = coords_of(brick, levels)

    near = []
    for axis in range(3):
        above, below = list(here), list(here)
        above[axis] = here[axis] + 1
        below[axis] = here[axis] + side - 1
        near.append((
            here[axis] < side - 1, (tomo, index_of(above, levels)),
            here[axis] > 0, (tomo, index_of(below, levels)),
        ))

    def mate_on(v, width):
        bit = lax.rem(v // width, 2)
        return bit, v + width - 2 * width * bit

    core = mate_on(brick, 1)
    core = (core[0], (tomo, core[1]))
    tomos = []
    for k in range(tb):
        bit, mate = mate_on(tomo, 1 << k)
        tomos.append((bit, (mate, brick)))
    rest = []
    for k in range(1, bb):
        bit, mate = mate_on(brick, 1 << k)
        rest.append((bit, (tomo, mate)))
    orders = ([core] + tomos + rest, [core] + tomos[::-1] + rest)
    stages = len(orders[0])

    barrier = pltpu.get_barrier_semaphore()
    count = stages
    for _, mate in orders[0]:
        pl.semaphore_signal(barrier, inc=1, device_id=mate, device_id_type=MESH)
    for has_above, above, has_below, below in near:
        for has, mate in ((has_above, above), (has_below, below)):

            @pl.when(has)
            def _(mate=mate):
                pl.semaphore_signal(barrier, inc=1, device_id=mate, device_id_type=MESH)

            count = count + has.astype(jnp.int32)

    slots = []
    for p in range(8):
        s = jnp.int32(0)
        for k in range(8):
            s = jnp.where(pos_ref[k] == p, k, s)
        slots.append(s)

    def gather(x, carry):
        for a, ref in ((0, f_ref), (1, g_ref)):
            for q in range(4):
                parts = []
                for pz in range(2):
                    s = slots[2 * q + pz]
                    v = ref[s, x].astype(jnp.float32)
                    parts.append(jnp.where(s < cnt_ref[0], v, 0.0))
                pad[a, 1, 1 + q // 2 * BE + x, pl.ds(1 + q % 2 * BE, BE)] = jnp.concatenate(
                    parts, axis=1
                ).astype(pad.dtype)
        return carry

    lax.fori_loop(0, BE, gather, 0)
    pl.semaphore_wait(barrier, count)

    def face(axis, at):
        if axis == 0:
            return pad.at[:, 1, at, pl.ds(1, e)]
        return pad.at[:, 1, :, at]

    def ends(axis):
        if axis == 2:
            return (zs.at[0], zr.at[0]), (zs.at[1], zr.at[1])
        return (face(axis, e), face(axis, 0)), (face(axis, 1), face(axis, e + 1))

    def halo_copies(axis):
        has_above, above, has_below, below = near[axis]
        up, down = ends(axis)
        made = []
        for k, (ends_k, mate) in enumerate(((up, above), (down, below))):
            made.append(pltpu.make_async_remote_copy(
                src_ref=ends_k[0], dst_ref=ends_k[1],
                send_sem=hsend.at[axis, k], recv_sem=hrecv.at[axis, k],
                device_id=mate, device_id_type=MESH,
            ))
        return made, (has_above, has_below)

    def halo_start(axis):
        made, has = halo_copies(axis)
        for k in range(2):

            @pl.when(has[k])
            def _(k=k):
                made[k].start()

    def halo_finish(axis):
        made, has = halo_copies(axis)
        for k in range(2):

            @pl.when(has[1 - k])
            def _(k=k):
                made[k].wait_recv()

            @pl.when(jnp.logical_not(has[1 - k]))
            def _(k=k):
                if axis == 0:
                    pad[:, 1, (0, e + 1)[k], pl.ds(1, e)] = jnp.zeros((2, e, e, ch), pad.dtype)
                elif axis == 1:
                    pad[:, 1, :, (0, e + 1)[k]] = jnp.zeros((2, e + 2, e, ch), pad.dtype)
                else:
                    zr[k] = jnp.zeros((2, e + 2, e + 2, ch), zr.dtype)

            @pl.when(has[k])
            def _(k=k):
                made[k].wait_send()

    halo_start(0)

    zero = jnp.zeros((ch, ch), wx.dtype)

    def spread(t, carry):
        ox, oz = t // 3, lax.rem(t, 3)
        for i in range(4):
            for p in range(2):
                oy = i - p
                at = (pl.ds(i * ch, ch), pl.ds(p * ch, ch))
                if 0 <= oy <= 2:
                    wx[(0, t) + at] = w_ref[ox * 9 + oy * 3 + oz]
                    wx[(1, t) + at] = w_ref[(2 - ox) * 9 + (2 - oy) * 3 + 2 - oz].T
                else:
                    wx[(0, t) + at] = zero
                    wx[(1, t) + at] = zero
        return carry

    lax.fori_loop(0, 9, spread, 0)
    halo_finish(0)
    halo_start(1)

    def turn(c, carry):
        for x in range(2):
            own = pad[1, 1, 2 * c + x + 1, pl.ds(1, e)].reshape(half, 2, e, ch)
            for p in range(2):
                gt[c, pl.ds(p * ch, ch), pl.ds(x * half * e, half * e)] = (
                    own[:, p].reshape(half * e, ch).T
                )
        return carry

    lax.fori_loop(0, half, turn, 0)
    halo_finish(1)

    def edges(x, carry):
        for a in range(2):
            v = pad[a, 1, x].astype(jnp.float32)
            zs[0, a, x] = v[:, e - 1]
            zs[1, a, x] = v[:, 0]
        return carry

    lax.fori_loop(0, e + 2, edges, 0)
    halo_start(2)
    halo_finish(2)

    zidx = lax.broadcasted_iota(jnp.int32, (1, e, 1), 1)

    def shift(a):
        def body(x, carry):
            mid = pad[a, 1, x].astype(jnp.float32)
            lo = zr[0, a, x][:, None, :]
            hi = zr[1, a, x][:, None, :]
            pad[a, 0, x] = jnp.where(zidx == 0, lo, pltpu.roll(mid, 1, 1)).astype(pad.dtype)
            pad[a, 2, x] = jnp.where(zidx == e - 1, hi, pltpu.roll(mid, e - 1, 1)).astype(pad.dtype)
            return carry

        lax.fori_loop(0, e + 2, body, 0)

    def rows(a, oz, x0, nx):
        v = pad[a, oz, pl.ds(x0, nx)].reshape(nx, half + 1, 2, e, ch)
        parts = [
            v[:, i // 2:i // 2 + half, i % 2].reshape(nx * half * e, ch) for i in range(4)
        ]
        return jnp.concatenate(parts, axis=1)

    def terms(t, carry):
        ox, oz = t // 3, lax.rem(t, 3)
        acc = jnp.zeros((2 * ch, 4 * ch), jnp.float32)
        for c in range(half):
            acc = acc + jnp.dot(
                gt[c], rows(0, oz, ox + 2 * c, 2), preferred_element_type=jnp.float32
            )
        for oy in range(3):
            block = acc[:ch, oy * ch:(oy + 1) * ch] + acc[ch:, (oy + 1) * ch:(oy + 2) * ch]
            src[pl.ds(pl.multiple_of((t * 3 + oy) * ch, ch), ch)] = block.T
        return carry

    routes = []
    spot = 0
    for base, size, order in streams:
        off = base
        route = []
        for bit, mate in orders[order]:
            size = size // 2
            route.append((
                pl.multiple_of(off + bit * size, UNIT),
                pl.multiple_of(off + size - bit * size, UNIT),
                size, spot, mate,
            ))
            off = off + bit * size
            spot += size
        routes.append(route)
    flying = {}

    def begin(s, j):
        down = j < stages
        k = j if down else 2 * stages - 1 - j
        keep, give, size, at, mate = routes[s][k]
        if down:
            copy = pltpu.make_async_remote_copy(
                src_ref=src.at[pl.ds(give, size)], dst_ref=land.at[pl.ds(at, size)],
                send_sem=rsend.at[s, k], recv_sem=rrecv.at[s, k],
                device_id=mate, device_id_type=MESH,
            )
        else:
            copy = pltpu.make_async_remote_copy(
                src_ref=tot.at[pl.ds(keep, size)], dst_ref=tot.at[pl.ds(keep, size)],
                send_sem=gsend.at[s, k], recv_sem=grecv.at[s, k],
                device_id=mate, device_id_type=MESH,
            )
        copy.start()
        flying[s] = copy

    def end(s, j):
        flying[s].wait()
        if j < stages:
            keep, give, size, at, mate = routes[s][j]
            both = src[pl.ds(keep, size)] + land[pl.ds(at, size)]
            if j < stages - 1:
                src[pl.ds(keep, size)] = both
            else:
                tot[pl.ds(keep, size)] = both * factor

    nx = 4

    def conv(a, c):
        x0 = c * nx
        acc = jnp.zeros((nx * half * e, 2 * ch), jnp.float32)
        for t in range(9):
            acc = acc + jnp.dot(
                rows(a, t % 3, x0 + t // 3, nx), wx[a, t], preferred_element_type=jnp.float32
            )
        for p in range(2):
            obuf[a, pl.ds(x0, nx), :, p] = (
                acc[:, p * ch:(p + 1) * ch].reshape(nx, half, 2, BE, ch).astype(obuf.dtype)
            )

    def put(a, dst):
        for s in range(8):
            p = pos_ref[s]
            v = obuf[
                a, pl.ds(p // 4 * BE, BE), pl.ds(lax.rem(p // 2, 2) * (BE // 2), BE // 2), :,
                lax.rem(p, 2),
            ].reshape(BE, BE, BE, ch)
            dst[s] = jnp.where(s < cnt_ref[0], v, jnp.zeros_like(v))

    work = []
    for a, dst in ((0, out_ref), (1, dx_ref)):
        if a == 1:
            work.append(functools.partial(shift, 1))
        for c in range(e // nx):
            work.append(functools.partial(conv, a, c))
        work.append(functools.partial(put, a, dst))

    lead = streams[2][0]
    early = min(9, -(-lead // (3 * ch)))
    first = (0, 1)
    second = (2, 3)
    used = 3 * 9 * ch
    shift(0)
    if src.shape[0] > used:
        src[pl.ds(used, src.shape[0] - used)] = jnp.zeros((src.shape[0] - used, ch), src.dtype)
    lax.fori_loop(0, early, terms, 0)
    for s in first:
        begin(s, 0)
    if early < 9:
        lax.fori_loop(early, 9, terms, 0)
    last = 2 * stages - 1
    skew = 1
    for tau in range(1, last + 2 + skew):
        for group, j in ((first, tau), (second, tau - skew)):
            for s in group:
                if 1 <= j <= last + 1:
                    end(s, j - 1)
                if 0 <= j <= last:
                    begin(s, j)
        for _ in range(1 if tau < last + skew else len(work)):
            if work:
                work.pop(0)()


def fused(features, cotangent, weight, pos, cnt, factor, n_tomo, n_brick):
    slots, vox, ch = features.shape
    e = 2 * BE
    half = e // 2
    n = n_tomo * n_brick
    tb, bb = n_tomo.bit_length() - 1, n_brick.bit_length() - 1
    stages = tb + bb
    rows = weight.shape[0] * ch
    unit = UNIT * n
    units = -(-rows // unit)
    units = max(units, 4)
    lead = 5 * 3 * ch // unit
    lead = min(lead, units // 2) if lead >= 2 else 2
    parts = [lead - lead // 2, lead // 2, units - lead - (units - lead) // 2, (units - lead) // 2]
    streams = []
    base = 0
    for k, u in enumerate(parts):
        streams.append((base, u * unit, k % 2))
        base += u * unit
    total = base
    vm = pl.BlockSpec(memory_space=pltpu.VMEM)
    sm = pl.BlockSpec(memory_space=pltpu.SMEM)
    brick = jax.ShapeDtypeStruct((slots, BE, BE, BE, ch), jnp.bfloat16)
    dma = pltpu.SemaphoreType.DMA
    out, dx, tot = pl.pallas_call(
        functools.partial(kernel, factor, tb, bb, streams),
        out_shape=(brick, brick, jax.ShapeDtypeStruct((total, ch), jnp.float32)),
        in_specs=[sm, sm, vm, vm, vm],
        out_specs=(vm, vm, vm),
        scratch_shapes=[
            pltpu.VMEM((2, 3, e + 2, e + 2, e, ch), jnp.bfloat16),
            pltpu.VMEM((2, 2, e + 2, e + 2, ch), jnp.float32),
            pltpu.VMEM((2, 2, e + 2, e + 2, ch), jnp.float32),
            pltpu.VMEM((2, 9, 4 * ch, 2 * ch), jnp.bfloat16),
            pltpu.VMEM((half, 2 * ch, 2 * half * e), jnp.bfloat16),
            pltpu.VMEM((2, e, half, 2, 2, BE, ch), jnp.bfloat16),
            pltpu.VMEM((total, ch), jnp.float32),
            pltpu.VMEM((total, ch), jnp.float32),
            dma((3, 2)), dma((3, 2)),
            dma((4, stages)), dma((4, stages)), dma((4, stages)), dma((4, stages)),
        ],
        compiler_params=pltpu.CompilerParams(
            collective_id=0, has_side_effects=True, vmem_limit_bytes=58 << 20
        ),
        name="fused",
    )(
        pos, cnt,
        features.reshape(slots, BE, BE, BE, ch), cotangent.reshape(slots, BE, BE, BE, ch), weight,
    )
    dw = tot[:rows].reshape(3, 3, 3, ch, ch).transpose(0, 2, 1, 3, 4).reshape(weight.shape)
    return out, dx, dw


def shards(features, weight, cotangent, brick_pos, brick_count):
    slots, vox, ch = features.shape[1:]
    n_tomo, n_brick = lax.axis_size("tomo"), lax.axis_size("brick")
    factor = 1.0 / math.sqrt(n_tomo * n_brick * slots * vox)
    out, dx, dw = fused(
        features[0], cotangent[0], weight, brick_pos[0], brick_count[0], factor, n_tomo, n_brick
    )
    return out.reshape(1, slots, vox, ch), dx.reshape(1, slots, vox, ch), dw


def solution(mesh):
    in_specs = (
        P("tomo", "brick", None, None),
        P(),
        P("tomo", "brick", None, None),
        P("tomo", "brick"),
        P("tomo", "brick"),
    )
    out_specs = (P("tomo", "brick", None, None), P("tomo", "brick", None, None), P())
    return jax.shard_map(shards, mesh=mesh, in_specs=in_specs, out_specs=out_specs, check_vma=False)
```

profile of v0, /device:TPU:0, one launch (start us, length us, event | category | flops | bytes accessed | tf_op | source)
XLA Modules:
  0.0 77.7 jit_solution(2369666242730681653)
XLA Ops:
  1.3 70.9 %fused.1 = (bf16[8,8,8,8,128]{4,3,2,1,0:T(8,128)(2,1)}, bf16[8,8,8,8,128]{4,3,2,1,0:T(8,128)(2,1)}, f32[3584,128]{1,0:T(8,128)}) custom-call(s32[8]{0:T(128)} %bitcast.17, s32[1]{0:T(128)} %bitcast.10.cnt_ref, bf16[8,8,8,8,128]{4,3,2,1,0:T(8,128)(2,1)} %bitcast.13, bf16[8,8,8,8,128]{4,3,2,1,0:T(8,128)(2,1)} %bitcast.14, bf16[27,128,128]{2,1,0:T(8,128)(2,1)} %w_ref.1), custom_call_target="tpu_custom_call" | custom-call | tf_op jit(solution)/shard_map/fused/pallas_call | solution.py:369
  72.1 1.6 %slice.3 = f32[3456,128]{1,0:T(8,128)S(1)} slice(f32[3584,128]{1,0:T(8,128)} %get-tuple-element.8), slice={[0:3456], [0:128]} | slice | bytes 3538944 | tf_op jit(solution)/shard_map/slice | solution.py:394
  73.7 0.0 copy-start.1
  73.7 1.4 %copy.8 = f32[3,3,3,128,128]{4,3,2,1,0:T(8,128)} copy(f32[3,3,3,128,128]{4,3,1,2,0:T(8,128)S(1)} %bitcast.11) | data formatting | bytes 3538944 | tf_op jit(solution)/shard_map/transpose | solution.py:394
  75.1 0.0 copy-start
  75.1 0.1 copy-done.1
  75.2 1.0 %copy.12 = bf16[1,8,512,128]{3,2,1,0:T(8,128)(2,1)} copy(bf16[1,8,512,128]{3,2,1,0:T(8,128)(2,1)S(1)} %bitcast.16) | data formatting | bytes 2097152
  76.2 0.6 copy-done
  76.8 1.0 %copy.13 = bf16[1,8,512,128]{3,2,1,0:T(8,128)(2,1)} copy(bf16[1,8,512,128]{3,2,1,0:T(8,128)(2,1)S(1)} %bitcast.15) | data formatting | bytes 2097152
Async XLA Ops:
  73.7 1.5 %copy-start.1 = (bf16[8,8,8,8,128]{4,3,2,1,0:T(8,128)(2,1)S(1)}, bf16[8,8,8,8,128]{4,3,2,1,0:T(8,128)(2,1)}, u32[]{:S(2)}) copy-start(bf16[8,8,8,8,128]{4,3,2,1,0:T(8,128)(2,1)} %get-tuple-element.6) | copy-start | bytes 3145732
  75.1 1.6 %copy-start = (bf16[8,8,8,8,128]{4,3,2,1,0:T(8,128)(2,1)S(1)}, bf16[8,8,8,8,128]{4,3,2,1,0:T(8,128)(2,1)}, u32[]{:S(2)}) copy-start(bf16[8,8,8,8,128]{4,3,2,1,0:T(8,128)(2,1)} %get-tuple-element.7) | copy-start | bytes 3145732
where the time goes:
time: 78 us; the launch traced here: 77.7 us
  Pallas kernels  70.9 us (91%)
  local copies, waits for them, and re-layouts  5.57 us (7%)
  between operations  1.3 us (2%)
    pallas_call x1, Pallas kernels, fused(): pl.pallas_call(functools.partial(kernel, factor, tb, bb, streams), out_sh...  70.9 us
    unnamed x6, local copies, waits for them, and re-layouts  2.59 us
    slice x1, local copies, waits for them, and re-layouts, fused(): tot[:rows].reshape(3, 3, 3, ch, ch).transpose(0, 2, 1, 3, 4)  1.59 us

commit v1 on v0

--- a/solution.py
+++ b/solution.py
@@ -34,8 +34,8 @@
 def kernel(
     factor, tb, bb, streams,
     pos_ref, cnt_ref, f_ref, g_ref, w_ref,
-    out_ref, dx_ref, tot,
-    pad, zs, zr, wx, gt, obuf, src, land,
+    out_ref, dx_ref, dw_ref,
+    pad, zs, zr, wx, gt, obuf, src, land, tot,
     hsend, hrecv, rsend, rrecv, gsend, grecv,
 ):
     e = 2 * BE
@@ -110,38 +110,38 @@
     lax.fori_loop(0, BE, gather, 0)
     pl.semaphore_wait(barrier, count)
 
-    def face(axis, at):
+    def face(axis, a, at):
         if axis == 0:
-            return pad.at[:, 1, at, pl.ds(1, e)]
-        return pad.at[:, 1, :, at]
-
-    def ends(axis):
+            return pad.at[a, 1, at, pl.ds(1, e)]
+        return pad.at[a, 1, :, at]
+
+    def ends(axis, a):
         if axis == 2:
-            return (zs.at[0], zr.at[0]), (zs.at[1], zr.at[1])
-        return (face(axis, e), face(axis, 0)), (face(axis, 1), face(axis, e + 1))
-
-    def halo_copies(axis):
+            return (zs.at[0, a], zr.at[0, a]), (zs.at[1, a], zr.at[1, a])
+        return (face(axis, a, e), face(axis, a, 0)), (face(axis, a, 1), face(axis, a, e + 1))
+
+    def halo_copies(axis, a):
         has_above, above, has_below, below = near[axis]
-        up, down = ends(axis)
+        up, down = ends(axis, a)
         made = []
         for k, (ends_k, mate) in enumerate(((up, above), (down, below))):
             made.append(pltpu.make_async_remote_copy(
                 src_ref=ends_k[0], dst_ref=ends_k[1],
-                send_sem=hsend.at[axis, k], recv_sem=hrecv.at[axis, k],
+                send_sem=hsend.at[axis, a, k], recv_sem=hrecv.at[axis, a, k],
                 device_id=mate, device_id_type=MESH,
             ))
         return made, (has_above, has_below)
 
-    def halo_start(axis):
-        made, has = halo_copies(axis)
+    def halo_start(axis, a):
+        made, has = halo_copies(axis, a)
         for k in range(2):
 
             @pl.when(has[k])
             def _(k=k):
                 made[k].start()
 
-    def halo_finish(axis):
-        made, has = halo_copies(axis)
+    def halo_finish(axis, a):
+        made, has = halo_copies(axis, a)
         for k in range(2):
 
             @pl.when(has[1 - k])
@@ -151,17 +151,18 @@
             @pl.when(jnp.logical_not(has[1 - k]))
             def _(k=k):
                 if axis == 0:
-                    pad[:, 1, (0, e + 1)[k], pl.ds(1, e)] = jnp.zeros((2, e, e, ch), pad.dtype)
+                    pad[a, 1, (0, e + 1)[k], pl.ds(1, e)] = jnp.zeros((e, e, ch), pad.dtype)
                 elif axis == 1:
-                    pad[:, 1, :, (0, e + 1)[k]] = jnp.zeros((2, e + 2, e, ch), pad.dtype)
+                    pad[a, 1, :, (0, e + 1)[k]] = jnp.zeros((e + 2, e, ch), pad.dtype)
                 else:
-                    zr[k] = jnp.zeros((2, e + 2, e + 2, ch), zr.dtype)
+                    zr[k, a] = jnp.zeros((e + 2, e + 2, ch), zr.dtype)
 
             @pl.when(has[k])
             def _(k=k):
                 made[k].wait_send()
 
-    halo_start(0)
+    halo_start(0, 0)
+    halo_start(0, 1)
 
     zero = jnp.zeros((ch, ch), wx.dtype)
 
@@ -180,8 +181,8 @@
         return carry
 
     lax.fori_loop(0, 9, spread, 0)
-    halo_finish(0)
-    halo_start(1)
+    halo_finish(0, 0)
+    halo_start(1, 0)
 
     def turn(c, carry):
         for x in range(2):
@@ -193,18 +194,22 @@
         return carry
 
     lax.fori_loop(0, half, turn, 0)
-    halo_finish(1)
-
-    def edges(x, carry):
-        for a in range(2):
+    halo_finish(1, 0)
+
+    def edges(a):
+        def body(x, carry):
             v = pad[a, 1, x].astype(jnp.float32)
             zs[0, a, x] = v[:, e - 1]
             zs[1, a, x] = v[:, 0]
-        return carry
-
-    lax.fori_loop(0, e + 2, edges, 0)
-    halo_start(2)
-    halo_finish(2)
+            return carry
+
+        lax.fori_loop(0, e + 2, body, 0)
+
+    edges(0)
+    halo_start(2, 0)
+    halo_finish(0, 1)
+    halo_start(1, 1)
+    halo_finish(2, 0)
 
     zidx = lax.broadcasted_iota(jnp.int32, (1, e, 1), 1)
 
@@ -310,6 +315,7 @@
     work = []
     for a, dst in ((0, out_ref), (1, dx_ref)):
         if a == 1:
+            work.append(functools.partial(halo_finish, 2, 1))
             work.append(functools.partial(shift, 1))
         for c in range(e // nx):
             work.append(functools.partial(conv, a, c))
@@ -326,10 +332,13 @@
     lax.fori_loop(0, early, terms, 0)
     for s in first:
         begin(s, 0)
+    halo_finish(1, 1)
+    edges(1)
+    halo_start(2, 1)
     if early < 9:
         lax.fori_loop(early, 9, terms, 0)
     last = 2 * stages - 1
-    skew = 1
+    skew = 2
     for tau in range(1, last + 2 + skew):
         for group, j in ((first, tau), (second, tau - skew)):
             for s in group:
@@ -340,6 +349,15 @@
         for _ in range(1 if tau < last + skew else len(work)):
             if work:
                 work.pop(0)()
+
+    def lay(t, carry):
+        for oy in range(3):
+            dw_ref[t // 3 * 9 + oy * 3 + lax.rem(t, 3)] = tot[
+                pl.ds(pl.multiple_of((t * 3 + oy) * ch, ch), ch)
+            ]
+        return carry
+
+    lax.fori_loop(0, 9, lay, 0)
 
 
 def fused(features, cotangent, weight, pos, cnt, factor, n_tomo, n_brick):
@@ -366,9 +384,9 @@
     sm = pl.BlockSpec(memory_space=pltpu.SMEM)
     brick = jax.ShapeDtypeStruct((slots, BE, BE, BE, ch), jnp.bfloat16)
     dma = pltpu.SemaphoreType.DMA
-    out, dx, tot = pl.pallas_call(
+    return pl.pallas_call(
         functools.partial(kernel, factor, tb, bb, streams),
-        out_shape=(brick, brick, jax.ShapeDtypeStruct((total, ch), jnp.float32)),
+        out_shape=(brick, brick, jax.ShapeDtypeStruct(weight.shape, jnp.float32)),
         in_specs=[sm, sm, vm, vm, vm],
         out_specs=(vm, vm, vm),
         scratch_shapes=[
@@ -380,7 +398,8 @@
             pltpu.VMEM((2, e, half, 2, 2, BE, ch), jnp.bfloat16),
             pltpu.VMEM((total, ch), jnp.float32),
             pltpu.VMEM((total, ch), jnp.float32),
-            dma((3, 2)), dma((3, 2)),
+            pltpu.VMEM((total, ch), jnp.float32),
+            dma((3, 2, 2)), dma((3, 2, 2)),
             dma((4, stages)), dma((4, stages)), dma((4, stages)), dma((4, stages)),
         ],
         compiler_params=pltpu.CompilerParams(
@@ -391,8 +410,6 @@
         pos, cnt,
         features.reshape(slots, BE, BE, BE, ch), cotangent.reshape(slots, BE, BE, BE, ch), weight,
     )
-    dw = tot[:rows].reshape(3, 3, 3, ch, ch).transpose(0, 2, 1, 3, 4).reshape(weight.shape)
-    return out, dx, dw
 
 
 def shards(features, weight, cotangent, brick_pos, brick_count):

time: 78 us -> 74.2 us (0.951)
  Pallas kernels: 70.9 us -> 68.1 us
  local copies, waits for them, and re-layouts: 5.57 us -> 4.61 us
    pallas_call x1, Pallas kernels: 70.9 us -> 68.1 us  [fused(): pl.pallas_call(functools.partial(kernel, factor, tb, bb, streams), out_sh...]
    unnamed x6 -> x7, local copies, waits for them, and re-layouts: 2.59 us -> 4.61 us
    slice x1 -> x0, local copies, waits for them, and re-layouts: 1.59 us -> none  [fused(): tot[:rows].reshape(3, 3, 3, ch, ch).transpose(0, 2, 1, 3, 4)]
    transpose x1 -> x0, local copies, waits for them, and re-layouts: 1.4 us -> none  [fused(): tot[:rows].reshape(3, 3, 3, ch, ch).transpose(0, 2, 1, 3, 4)]
where the time goes in v1:
time: 74.2 us; the launch traced here: 74 us
  Pallas kernels  68.1 us (92%)
  local copies, waits for them, and re-layouts  4.61 us (6%)
  between operations  1.3 us (2%)
    pallas_call x1, Pallas kernels, fused(): pl.pallas_call(functools.partial(kernel, factor, tb, bb, streams), out_sh...  68.1 us
    unnamed x7, local copies, waits for them, and re-layouts  4.61 us

profile of v1, /device:TPU:0, one launch (start us, length us, event | category | flops | bytes accessed | tf_op | source)
XLA Modules:
  0.0 74.0 jit_solution(15507571942899727704)
XLA Ops:
  1.3 68.1 %fused.1 = (bf16[8,8,8,8,128]{4,3,2,1,0:T(8,128)(2,1)}, bf16[8,8,8,8,128]{4,3,2,1,0:T(8,128)(2,1)}, f32[27,128,128]{2,1,0:T(8,128)}) custom-call(s32[8]{0:T(128)} %bitcast.11, s32[1]{0:T(128)} %bitcast.6.cnt_ref, bf16[8,8,8,8,128]{4,3,2,1,0:T(8,128)(2,1)} %bitcast.7, bf16[8,8,8,8,128]{4,3,2,1,0:T(8,128)(2,1)} %bitcast.8, bf16[27,128,128]{2,1,0:T(8,128)(2,1)} %w_ref.1), custom_call_target="tpu_custom_call" | custom-call | tf_op jit(solution)/shard_map/fused/pallas_call | solution.py:387
  69.4 0.0 copy-start.1
  69.4 0.0 copy-start
  69.4 2.4 %copy.12 = bf16[1,8,512,128]{3,2,1,0:T(8,128)(2,1)} copy(bf16[1,8,512,128]{3,2,1,0:T(8,128)(2,1)} %bitcast.10) | data formatting | bytes 2097152
  71.8 0.0 copy-done.1
  71.8 1.0 %copy.13 = bf16[1,8,512,128]{3,2,1,0:T(8,128)(2,1)} copy(bf16[1,8,512,128]{3,2,1,0:T(8,128)(2,1)S(1)} %bitcast.9) | data formatting | bytes 2097152
  72.8 0.0 copy-done
  72.8 1.2 %copy.14 = f32[27,128,128]{2,1,0:T(8,128)} copy(f32[27,128,128]{2,1,0:T(8,128)S(1)} %copy-done) | data formatting | bytes 3538944
Async XLA Ops:
  69.4 2.4 %copy-start.1 = (bf16[8,8,8,8,128]{4,3,2,1,0:T(8,128)(2,1)S(1)}, bf16[8,8,8,8,128]{4,3,2,1,0:T(8,128)(2,1)}, u32[]{:S(2)}) copy-start(bf16[8,8,8,8,128]{4,3,2,1,0:T(8,128)(2,1)} %get-tuple-element.7) | copy-start | bytes 3145732
  69.4 3.4 %copy-start = (f32[27,128,128]{2,1,0:T(8,128)S(1)}, f32[27,128,128]{2,1,0:T(8,128)}, u32[]{:S(2)}) copy-start(f32[27,128,128]{2,1,0:T(8,128)} %get-tuple-element.14) | copy-start | bytes 5308420
